TPU v7x, 1024 devices: a whole 4x8x16 slice. The times are simulated.
1024 devices in a mesh: worker: 64 (over y, z_lo, core), fsdp: 16 (over z_hi, x).
Axes of the slice: x: 4, y: 8, z: 16 (z_hi: 4, z_lo: 4; z = z_hi * 4 + z_lo), core: 2. Of those that a mesh axis runs over, the one named last changes fastest.
Arguments:
- tokens: bfloat16 [16384, 8192], P('worker', 'fsdp'), may hold values from -6 to 6
- inner_weight: bfloat16 [64, 8192, 512], P('worker', 'fsdp'), may hold values from -0.0625 to 0.0625
- key_grad: bfloat16 [16384, 512], P(('worker', 'fsdp')), may hold values from -6 to 6
- anchor: float32 [8192, 512], P('fsdp'), may hold values from -0.0625 to 0.0625
- momentum: float32 [8192, 512], P('fsdp'), may hold values from -0.06 to 0.06
- stale_delta: bfloat16 [64, 8192, 512], P('worker', 'fsdp'), may hold values from -0.29882812 to 0.29882812
Outputs:
- keys: bfloat16 [16384, 512], P(('worker', 'fsdp'))
- input_grad: bfloat16 [16384, 8192], P('worker', 'fsdp')
- new_params: bfloat16 [64, 8192, 512], P('worker', 'fsdp')
- new_momentum: float32 [8192, 512], P(('fsdp', 'worker'))
- fresh_delta: bfloat16 [64, 8192, 512], P('worker', 'fsdp')
All inputs are finite; a program needn't handle non-finite values.
Results may differ from a plain program's by a relative error of at most 0.001.
Values may be sent and summed in bfloat16 or wider, within the bound.
A program may use at most 32 MiB of HBM per device.

v0:
```python
import jax
import jax.numpy as jnp
from jax import lax
from jax.sharding import PartitionSpec as P

inner_rate = 0.0005
outer_rate = 0.7
outer_momentum = 0.9


def local(tokens, inner_weight, key_grad, anchor, momentum, stale_delta):
    weights = inner_weight[0]
    inputs = tokens
    key_out = lax.psum_scatter(
        jnp.dot(inputs, weights, preferred_element_type=jnp.float32),
        "fsdp",
        scatter_dimension=0,
        tiled=True,
    ).astype(jnp.bfloat16)
    portion = lax.all_gather(key_grad, "fsdp", axis=0, tiled=True)
    inputs = tokens
    grad_weight = lax.dot_general(
        inputs, portion, (((0,), (0,)), ((), ())), preferred_element_type=jnp.float32
    )
    product = lax.dot_general(
        portion, weights, (((1,), (1,)), ((), ())), preferred_element_type=jnp.float32
    )
    grad_input = product
    grad_weight, grad_input = (grad_weight, grad_input)
    fresh_term = anchor - (weights.astype(jnp.float32) - inner_rate * grad_weight)
    stale_value = stale_delta[0].astype(jnp.float32)
    workers = lax.axis_size("worker")
    share_rows = anchor.shape[0] // workers
    worker_index = lax.axis_index("worker")
    summed = lax.psum(stale_value, "worker")
    average = summed / workers
    moment_full = outer_momentum * momentum + average
    common_term = average + outer_momentum * moment_full
    new_moment = lax.dynamic_slice_in_dim(moment_full, worker_index * share_rows, share_rows, 0)
    updated = anchor - outer_rate * (common_term + (fresh_term - stale_value) / workers)
    fresh_out = fresh_term[None].astype(jnp.bfloat16)
    return (
        key_out,
        grad_input.astype(jnp.bfloat16),
        updated[None].astype(jnp.bfloat16),
        new_moment,
        fresh_out,
    )


def solution(mesh):
    in_specs = (
        P("worker", "fsdp"),
        P("worker", "fsdp", None),
        P(("worker", "fsdp"), None),
        P("fsdp", None),
        P("fsdp", None),
        P("worker", "fsdp", None),
    )
    out_specs = (
        P(("worker", "fsdp"), None),
        P("worker", "fsdp"),
        P("worker", "fsdp", None),
        P(("fsdp", "worker"), None),
        P("worker", "fsdp", None),
    )
    return jax.shard_map(local, mesh=mesh, in_specs=in_specs, out_specs=out_specs, check_vma=False)
```

profile of v0, /device:TPU:1, one launch (start us, length us, event | category | flops | bytes accessed | tf_op | source)
XLA Modules:
  0.0 591.9 jit_solution(8182767852307067915)
XLA Ops:
  8.0 0.0 copy-start
  8.0 0.0 all-reduce.2.cloned.1.call-start
  8.1 2.2 bitcast_convert_fusion
  10.3 0.0 copy-start.1
  10.3 0.0 all-reduce.2.cloned.1.call-update
  10.3 0.0 reduce-scatter.2.cloned.1.call-start
  10.4 0.0 copy-done
  10.4 1.0 copy-done.1
  11.3 0.0 copy-start.4
  11.3 1.1 fusion.4
  12.5 0.0 copy-start.3
  12.5 0.0 reduce-scatter.2.cloned.1.call-update
  12.5 0.0 copy-done.4
  12.5 59.2 %all_gather.3 = bf16[256,512]{1,0:T(8,128)(2,1)S(1)} all-gather(bf16[16,512]{1,0:T(8,128)(2,1)S(1)} %copy-done.4), channel_id=1, replica_groups=mesh['worker'=64,'fsdp'=16] {'fsdp'}, dimensions={0}, use_global_device_ids=true | all-gather | bytes 278528 | tf_op jit(solution)/shard_map/all_gather | solution.py:20
  71.7 0.0 copy-start.2
  71.7 1.0 convolution_convert_fusion
  72.8 506.5 %all-reduce.2.cloned.1.call-done = f32[512,512]{1,0:T(8,128)} async-done(((f32[512,512]{1,0:T(8,128)}), f32[512,512]{1,0:T(8,128)}) %all-reduce.2.cloned.1.call-update) | async-done | bytes 1048592 | tf_op jit(solution)/shard_map/psum | solution.py:35
  579.2 0.0 copy-done.3
  579.2 0.0 copy-done.2
  579.2 3.2 multiply_add_fusion
  582.5 0.6 constant_dynamic-slice_fusion
  583.1 0.0 reduce-scatter.2.cloned.1.call-done
  583.1 1.4 convert_element_type.27
Async XLA Ops:
  8.0 2.4 copy-start
  8.0 571.2 %all-reduce.2.cloned.1.call-start = ((), (), s32[]{:S(2)}) async-start(), calls=%async_computation.2 | async-start | bytes 2097152 | tf_op jit(solution)/shard_map/psum | solution.py:35
  10.3 1.0 copy-start.1
  10.3 572.7 %reduce-scatter.2.cloned.1.call-start = ((), (), s32[]{:S(2)}) async-start(), calls=%async_computation.1 | async-start | bytes 557056 | tf_op jit(solution)/shard_map/reduce_scatter | solution.py:14
  11.3 1.1 copy-start.4
  12.5 566.8 %copy-start.3 = (f32[512,512]{1,0:T(8,128)S(1)}, f32[512,512]{1,0:T(8,128)}, u32[]{:S(2)}) copy-start(f32[512,512]{1,0:T(8,128)} %param.10) | copy-start | bytes 3145732
  71.7 507.5 %copy-start.2 = (bf16[1,512,512]{2,1,0:T(8,128)(2,1)S(1)}, bf16[1,512,512]{2,1,0:T(8,128)(2,1)}, u32[]{:S(2)}) copy-start(bf16[1,512,512]{2,1,0:T(8,128)(2,1)} %param.11) | copy-start | bytes 1572868
Sparse Core Ops, SparseCore 0:
  12.3 566.8 all-reduce.1
Sparse Core Ops, SparseCore 1:
  16.0 127.4 reduce-scatter.1
where the time goes:
time: 592 us
  waiting for transfers between devices  507 us (86%)
  blocking collectives  59.2 us (10%)
  between operations  15.5 us (3%)
    psum x1, waiting for transfers between devices, local(): summed = lax.psum(stale_value, 'worker')  506 us
    all_gather x1, blocking collectives, local(): portion = lax.all_gather(key_grad, 'fsdp', axis=0, tiled=True)  59.2 us
  transfers between devices with their start and end apart: 2, of which 1 were waited for; matrix products, arithmetic and copies ran while one was open for 1% of the time, Pallas kernels for 0%

commit v1 on v0

v1 whole, which is shorter than its diff:
```python
import jax
import jax.numpy as jnp
from jax import lax
from jax.experimental import pallas as pl
from jax.experimental.pallas import tpu as pltpu
from jax.sharding import PartitionSpec as P

inner_rate = 0.0005
outer_rate = 0.7
outer_momentum = 0.9

Y, ZL, C, ZH, X = 8, 4, 2, 4, 4
WORKERS = Y * ZL * C
ROWS, KW, TOK = 512, 512, 256
HALF = ROWS // C
CH = HALF // Y
J = 2
R = CH // J
SH = 16
F32, BF16 = jnp.float32, jnp.bfloat16
MESH = pl.DeviceIdType.MESH


class Ids:
    def __init__(self):
        self.n = 0

    def __call__(self, *shape):
        first, self.n = self.n, self.n + _size(shape)

        def at(*index):
            k = 0
            for i, s in zip(index, shape):
                k = k * s + i
            return first + k

        return at


def _size(shape):
    n = 1
    for s in shape:
        n *= s
    return n


ids = Ids()
ID_PAIR = ids(Y)
ID_RS = ids(J, 2, Y // 2)
ID_Z = ids(J, ZL - 1)
ID_AG = ids(J, 2, Y // 2)
ID_PAG = ids(Y, J)
ID_KZ = ids(3)
ID_KX = ids(4, X - 1)
ID_PX = ids(X - 1)
ID_PZ = ids(3)
N_REMOTE = ids.n

loc = Ids()
L_STALE, L_W, L_TOK, L_ANCHOR, L_MOM, L_KG = (loc(1)() for _ in range(6))
L_KEYS, L_IG, L_FRESH, L_NM = (loc(1)() for _ in range(4))
L_NEW = loc(2 * Y)
N_LOCAL = loc.n


def kernel(
    tok_ref, w_ref, kg_ref, anchor_ref, mom_ref, stale_ref,
    keys_ref, ig_ref, new_ref, nm_ref, fresh_ref,
    stale, wv, tok, anchor, mom, pair, acc, rs, zbuf, full, pre,
    kg, part, xbuf, ksum, zb, ig, fbuf, nbuf, keys, nm,
    ss, rr, ls,
):
    w = lax.axis_index("worker")
    f = lax.axis_index("fsdp")
    c, zl, y = w % C, (w // C) % ZL, w // (C * ZL)
    x, zh = f % X, f // X
    d = 1 - 2 * c

    def dev(y=y, zl=zl, c=c, zh=zh, x=x):
        return ((y * ZL + zl) * C + c, zh * X + x)

    def wrap(v, n):
        return (v + n) % n

    partner = dev(c=1 - c)
    ynext = {1: dev(y=wrap(y + 1, Y)), -1: dev(y=wrap(y - 1, Y))}
    zpeer = [dev(zl=wrap(zl + k, ZL)) for k in range(1, ZL)]
    xpeer = [dev(x=wrap(x + k, X)) for k in range(1, X)]
    zfwd, zbwd = dev(zh=wrap(zh + d, ZH)), dev(zh=wrap(zh - d, ZH))

    barrier = pltpu.get_barrier_semaphore()
    peers = [partner, ynext[1], ynext[-1], *zpeer, *xpeer, zfwd, zbwd]
    for peer in peers:
        pl.semaphore_signal(barrier, inc=1, device_id=peer, device_id_type=MESH)

    def load(src, dst, at):
        copy = pltpu.make_async_copy(src, dst, ls.at[at])
        copy.start()
        return copy

    h0, h1 = pl.multiple_of(c * HALF, HALF), pl.multiple_of((1 - c) * HALF, HALF)
    c_w = load(w_ref.at[0], wv, L_W)
    c_tok = load(tok_ref, tok, L_TOK)
    c_stale = load(stale_ref.at[0], stale, L_STALE)
    c_kg = load(kg_ref, kg.at[f], L_KG)
    c_anchor = load(anchor_ref, anchor, L_ANCHOR)
    c_mom = load(mom_ref, mom, L_MOM)

    sent = []

    def send(src, dst, at, to):
        copy = pltpu.make_async_remote_copy(
            src_ref=src, dst_ref=dst, send_sem=ss.at[at], recv_sem=rr.at[at],
            device_id=to, device_id_type=MESH,
        )
        copy.start()
        sent.append(copy)

    def got(dst, at):
        pltpu.make_async_remote_copy(
            src_ref=dst, dst_ref=dst, send_sem=ss.at[at], recv_sem=rr.at[at],
            device_id=partner, device_id_type=MESH,
        ).wait_recv()

    c_w.wait()
    c_tok.wait()
    for b in range(2):
        half = jnp.dot(tok[b * 128 : b * 128 + 128, :], wv[...], preferred_element_type=F32)
        for i in range(8):
            at = b * 8 + i
            part[at % X, at // X] = half[i * SH : (i + 1) * SH]
    pl.semaphore_wait(barrier, len(peers))

    order = [Y // 2] + [s * k for k in range(Y // 2 - 1, 0, -1) for s in (1, -1)] + [0]

    def chunk(o):
        return pl.multiple_of(wrap(y + o, Y) * CH, CH)

    for i, o in enumerate(order):
        at = chunk(o)
        send(stale_ref.at[0, pl.ds(h1 + at, CH)], pair.at[pl.ds(at, CH)], ID_PAIR(i), partner)

    send(kg_ref, kg.at[f], ID_KZ(0), zfwd)
    send(kg_ref, kg.at[f], ID_KZ(1), zbwd)
    for k in range(X - 1):
        send(kg_ref, kg.at[f], ID_KX(0, k), xpeer[k])
    for k in range(X - 1):
        send(part.at[wrap(x + k + 1, X)], xbuf.at[k], ID_PX(k), xpeer[k])

    def kshare(steps):
        return wrap(zh - d * steps + 4, ZH) * X + x

    def kg_from(steps, z_id, rel):
        at = kshare(steps)
        got(kg.at[at], ID_KZ(z_id))
        for k in range(X - 1):
            send(kg.at[at], kg.at[at], ID_KX(rel, k), xpeer[k])
        return at

    c_stale.wait()

    def hops(j, way):
        return Y // 2 if (j % 2 == 0) == (way == 1) else Y // 2 - 1

    def slot(j, way, s):
        return rs.at[j, 0 if way == 1 else 1, s]

    def rid(ident, j, way, s):
        return ident(j, 0 if way == 1 else 1, s)

    long_first = [(j, way) for n in (Y // 2, Y // 2 - 1) for j in range(J) for way in (1, -1) if hops(j, way) == n]
    for i, o in enumerate(order):
        at = chunk(o)
        got(pair.at[pl.ds(at, CH)], ID_PAIR(i))
        acc[pl.ds(at, CH), :] = stale[pl.ds(h0 + at, CH), :].astype(F32) + pair[pl.ds(at, CH), :].astype(F32)
        for j, way in long_first:
            if hops(j, way) * way == o or (o == Y // 2 and hops(j, way) == o):
                send(acc.at[pl.ds(at + j * R, R)], slot(j, way, 0), rid(ID_RS, j, way, 0), ynext[way])
    for s in range(1, Y // 2):
        for j, way in long_first:
            n = hops(j, way)
            if s < n:
                mine = slot(j, way, s - 1)
                got(mine, rid(ID_RS, j, way, s - 1))
                mine[...] = mine[...] + acc[pl.ds(chunk(way * (n - s)) + j * R, R), :]
                send(mine, slot(j, way, s), rid(ID_RS, j, way, s), ynext[way])
        if s == 1:
            kg_b = kg_from(1, 0, 1)
            send(kg.at[kg_b], kg.at[kg_b], ID_KZ(2), zfwd)
            kg_from(-1, 1, 2)

    for j in range(J):
        total = acc[pl.ds(chunk(0) + j * R, R), :]
        for way in (1, -1):
            n = hops(j, way)
            got(slot(j, way, n - 1), rid(ID_RS, j, way, n - 1))
            total = total + slot(j, way, n - 1)[...]
        zbuf[j, zl] = total
        for k in range(ZL - 1):
            send(zbuf.at[j, zl], zbuf.at[j, zl], ID_Z(j, k), zpeer[k])

    kg_from(2, 2, 3)
    for k in range(X - 1):
        got(xbuf.at[k], ID_PX(k))
    for i in range(ZH):
        ksum[i] = (part[x, i] + xbuf[0, i]) + (xbuf[1, i] + xbuf[2, i])
    send(ksum.at[wrap(zh + 2, ZH)], zb.at[0], ID_PZ(0), zfwd)
    send(ksum.at[wrap(zh - d, ZH)], zb.at[1], ID_PZ(1), zbwd)

    for rel, steps in enumerate((0, 1, -1, 2)):
        for k in range(X - 1):
            at = wrap(zh - d * steps + 4, ZH) * X + wrap(x - k - 1, X)
            got(kg.at[at], ID_KX(rel, k))
    c_kg.wait()
    portion = kg[...].reshape(TOK, KW)
    for b in range(2):
        ig[b * 128 : b * 128 + 128, :] = lax.dot_general(
            portion[b * 128 : b * 128 + 128], wv[...], (((1,), (1,)), ((), ())), preferred_element_type=F32
        ).astype(BF16)
    c_ig = load(ig, ig_ref, L_IG)
    c_anchor.wait()
    c_mom.wait()
    for b in range(4):
        rows = slice(b * 128, b * 128 + 128)
        grad = lax.dot_general(
            tok[:, rows], portion, (((0,), (0,)), ((), ())), preferred_element_type=F32
        )
        fresh = anchor[rows, :] - (wv[rows, :].astype(F32) - inner_rate * grad)
        fbuf[rows, :] = fresh.astype(BF16)
        pre[rows, :] = anchor[rows, :] - outer_rate * (
            outer_momentum * outer_momentum * mom[rows, :] + (fresh - stale[rows, :].astype(F32)) * (1.0 / WORKERS)
        )
    c_fresh = load(fbuf, fresh_ref.at[0], L_FRESH)

    def place(core, o, j):
        return pl.ds(pl.multiple_of(core * HALF + chunk(o) + j * R, R), R)

    for j in range(J):
        for k in range(ZL - 1):
            got(zbuf.at[j, wrap(zl - k - 1, ZL)], ID_Z(j, k))
        here = place(c, 0, j)
        full[here, :] = ((zbuf[j, 0] + zbuf[j, 1]) + (zbuf[j, 2] + zbuf[j, 3])) * (1.0 / WORKERS)
        for way in (1, -1):
            send(full.at[here], full.at[here], rid(ID_AG, j, way, 0), ynext[way])
        send(full.at[here], full.at[here], ID_PAG(0, j), partner)

    outs = []

    def finish(core, o, n):
        rows = pl.ds(pl.multiple_of(core * HALF + chunk(o), CH), CH)
        nbuf[rows, :] = (pre[rows, :] - (outer_rate * (1.0 + outer_momentum)) * full[rows, :]).astype(BF16)
        outs.append(load(nbuf.at[rows], new_ref.at[0, rows], L_NEW(n)))

    finish(c, 0, 0)
    for s in range(Y // 2):
        for j, way in long_first:
            n = hops(j, way)
            if s < n:
                o = -way * (s + 1)
                here = place(c, o, j)
                got(full.at[here], rid(ID_AG, j, way, s))
                if s + 1 < n:
                    send(full.at[here], full.at[here], rid(ID_AG, j, way, s + 1), ynext[way])
                send(full.at[here], full.at[here], ID_PAG(o % Y, j), partner)
        if s == 0:
            got(zb.at[0], ID_PZ(0))
            zb[0] = zb[0] + ksum[wrap(zh + d, ZH)]
            send(zb.at[0], zb.at[2], ID_PZ(2), zfwd)
        for o in (s + 1, -s - 1) if s + 1 < Y // 2 else (s + 1,):
            finish(c, o, o % Y)
        for o in (s, -s) if s else (0,):
            for j in range(J):
                got(full.at[place(1 - c, o, j)], ID_PAG(o % Y, j))
            finish(1 - c, o, Y + o % Y)
    got(zb.at[1], ID_PZ(1))
    got(zb.at[2], ID_PZ(2))
    keys[...] = (ksum[zh] + (zb[1] + zb[2])).astype(BF16)
    c_keys = load(keys, keys_ref, L_KEYS)
    for j in range(J):
        got(full.at[place(1 - c, Y // 2, j)], ID_PAG(Y // 2, j))
    finish(1 - c, Y // 2, Y + Y // 2)
    share = pl.ds(pl.multiple_of(w * 8, 8), 8)
    nm[...] = outer_momentum * mom[share, :] + full[share, :]
    c_nm = load(nm, nm_ref, L_NM)

    for copy in sent:
        copy.wait_send()
    for copy in (c_ig, c_fresh, c_keys, c_nm, *outs):
        copy.wait()


def local(*args):
    scratch = [
        pltpu.VMEM((ROWS, KW), BF16),
        pltpu.VMEM((ROWS, KW), BF16),
        pltpu.VMEM((TOK, ROWS), BF16),
        pltpu.VMEM((ROWS, KW), F32),
        pltpu.VMEM((ROWS, KW), F32),
        pltpu.VMEM((HALF, KW), BF16),
        pltpu.VMEM((HALF, KW), F32),
        pltpu.VMEM((J, 2, Y // 2, R, KW), F32),
        pltpu.VMEM((J, ZL, R, KW), F32),
        pltpu.VMEM((ROWS, KW), F32),
        pltpu.VMEM((ROWS, KW), F32),
        pltpu.VMEM((ZH * X, SH, KW), BF16),
        pltpu.VMEM((X, ZH, SH, KW), F32),
        pltpu.VMEM((X - 1, ZH, SH, KW), F32),
        pltpu.VMEM((ZH, SH, KW), F32),
        pltpu.VMEM((3, SH, KW), F32),
        pltpu.VMEM((TOK, ROWS), BF16),
        pltpu.VMEM((ROWS, KW), BF16),
        pltpu.VMEM((ROWS, KW), BF16),
        pltpu.VMEM((SH, KW), BF16),
        pltpu.VMEM((8, KW), F32),
        pltpu.SemaphoreType.DMA((N_REMOTE,)),
        pltpu.SemaphoreType.DMA((N_REMOTE,)),
        pltpu.SemaphoreType.DMA((N_LOCAL,)),
    ]
    hbm = pl.BlockSpec(memory_space=pl.ANY)
    return pl.pallas_call(
        kernel,
        out_shape=(
            jax.ShapeDtypeStruct((SH, KW), BF16),
            jax.ShapeDtypeStruct((TOK, ROWS), BF16),
            jax.ShapeDtypeStruct((1, ROWS, KW), BF16),
            jax.ShapeDtypeStruct((8, KW), F32),
            jax.ShapeDtypeStruct((1, ROWS, KW), BF16),
        ),
        in_specs=[hbm] * 6,
        out_specs=(hbm,) * 5,
        scratch_shapes=scratch,
        compiler_params=pltpu.CompilerParams(
            collective_id=0, has_side_effects=True, vmem_limit_bytes=60 * 1024 * 1024
        ),
    )(*args)


def solution(mesh):
    in_specs = (
        P("worker", "fsdp"),
        P("worker", "fsdp", None),
        P(("worker", "fsdp"), None),
        P("fsdp", None),
        P("fsdp", None),
        P("worker", "fsdp", None),
    )
    out_specs = (
        P(("worker", "fsdp"), None),
        P("worker", "fsdp"),
        P("worker", "fsdp", None),
        P(("fsdp", "worker"), None),
        P("worker", "fsdp", None),
    )
    return jax.shard_map(local, mesh=mesh, in_specs=in_specs, out_specs=out_specs, check_vma=False)
```

time: 592 us -> 64.7 us (0.11)
  waiting for transfers between devices: 507 us -> 0 us
  blocking collectives: 59.2 us -> 0 us
  Pallas kernels: 0 us -> 58.6 us
  between operations: 15.5 us -> 0.65 us
    psum x1 -> x0, waiting for transfers between devices: 506 us -> none  [local(): summed = lax.psum(stale_value, 'worker')]
    all_gather x1 -> x0, blocking collectives: 59.2 us -> none  [local(): portion = lax.all_gather(key_grad, 'fsdp', axis=0, tiled=True)]
    pallas_call x0 -> x1, Pallas kernels: none -> 58.6 us  [local(): pl.pallas_call(kernel, out_shape=(jax.ShapeDtypeStruct((SH, KW), BF16), j...]
  transfers between devices with their start and end apart: 2 -> 0, of which waited for: 1 -> 0; matrix products, arithmetic and copies ran while one was open for 1% -> 0% of each run, Pallas kernels for 0% -> 0%
where the time goes in v1:
time: 64.7 us; the launch traced here: 64.5 us
  Pallas kernels  58.6 us (91%)
  local copies, waits for them, and re-layouts  5.25 us (8%)
  between operations  0.65 us (1%)
    pallas_call x1, Pallas kernels, local(): pl.pallas_call(kernel, out_shape=(jax.ShapeDtypeStruct((SH, KW), BF16), j...  58.6 us
    unnamed x11, local copies, waits for them, and re-layouts  5.25 us

profile of v1, /device:TPU:1, one launch (start us, length us, event | category | flops | bytes accessed | tf_op | source)
XLA Modules:
  0.0 64.5 jit_solution(7899155365382989785)
XLA Ops:
  0.6 58.6 %shard_map.101 = (bf16[16,512]{1,0:T(8,128)(2,1)}, bf16[256,512]{1,0:T(8,128)(2,1)}, bf16[1,512,512]{2,1,0:T(8,128)(2,1)}, f32[8,512]{1,0:T(8,128)}, bf16[1,512,512]{2,1,0:T(8,128)(2,1)}) custom-call(bf16[256,512]{1,0:T(8,128)(2,1)} %tok_ref.1, bf16[1,512,512]{2,1,0:T(8,128)(2,1)} %w_ref.1, bf16[16,512]{1,0:T(8,128)(2,1)} %kg_ref.1, f32[512,512]{1,0:T(8,128)} %anchor_ref.1, ...), custom_call_target="tpu_custom_call" | custom-call | tf_op jit(solution)/shard_map/pallas_call | solution.py:320
  59.2 0.0 copy-start.1
  59.2 1.4 %copy.16 = bf16[16,512]{1,0:T(8,128)(2,1)} copy(bf16[16,512]{1,0:T(8,128)(2,1)} %get-tuple-element.10) | data formatting | bytes 32768
  60.6 1.7 %copy.17 = bf16[256,512]{1,0:T(8,128)(2,1)} copy(bf16[256,512]{1,0:T(8,128)(2,1)} %get-tuple-element.11) | data formatting | bytes 524288
  62.3 0.0 copy-done.1
  62.3 0.0 copy-start.2
  62.3 0.0 copy-start
  62.3 0.8 %copy.18 = bf16[1,512,512]{2,1,0:T(8,128)(2,1)} copy(bf16[1,512,512]{2,1,0:T(8,128)(2,1)S(1)} %copy-done.1) | data formatting | bytes 1048576
  63.1 0.0 copy-done.2
  63.1 0.6 copy.19
  63.7 0.0 copy-done
  63.7 0.8 %copy.20 = bf16[1,512,512]{2,1,0:T(8,128)(2,1)} copy(bf16[1,512,512]{2,1,0:T(8,128)(2,1)S(1)} %copy-done) | data formatting | bytes 1048576
Async XLA Ops:
  59.2 3.1 %copy-start.1 = (bf16[1,512,512]{2,1,0:T(8,128)(2,1)S(1)}, bf16[1,512,512]{2,1,0:T(8,128)(2,1)}, u32[]{:S(2)}) copy-start(bf16[1,512,512]{2,1,0:T(8,128)(2,1)} %get-tuple-element.12) | copy-start | bytes 1572868
  62.3 0.8 %copy-start.2 = (f32[8,512]{1,0:T(8,128)S(1)}, f32[8,512]{1,0:T(8,128)}, u32[]{:S(2)}) copy-start(f32[8,512]{1,0:T(8,128)} %get-tuple-element.13) | copy-start | bytes 49156
  62.3 1.4 %copy-start = (bf16[1,512,512]{2,1,0:T(8,128)(2,1)S(1)}, bf16[1,512,512]{2,1,0:T(8,128)(2,1)}, u32[]{:S(2)}) copy-start(bf16[1,512,512]{2,1,0:T(8,128)(2,1)} %get-tuple-element.14) | copy-start | bytes 1572868

commit v2 on v1

v2 whole, which is shorter than its diff:
```python
import jax
import jax.numpy as jnp
from jax import lax
from jax.experimental import pallas as pl
from jax.experimental.pallas import tpu as pltpu
from jax.sharding import PartitionSpec as P

inner_rate = 0.0005
outer_rate = 0.7
outer_momentum = 0.9

Y, ZL, C, ZH, X = 8, 4, 2, 4, 4
WORKERS = Y * ZL * C
ROWS, KW, TOK = 512, 512, 256
HALF = ROWS // C
CH = HALF // Y
J = 2
R = CH // J
SH = 16
VMEM_LIMIT = 53400 * 1024
F32, BF16 = jnp.float32, jnp.bfloat16
MESH = pl.DeviceIdType.MESH


class Ids:
    def __init__(self):
        self.n = 0

    def __call__(self, *shape):
        first, self.n = self.n, self.n + _size(shape)

        def at(*index):
            k = 0
            for i, s in zip(index, shape):
                k = k * s + i
            return first + k

        return at


def _size(shape):
    n = 1
    for s in shape:
        n *= s
    return n


ids = Ids()
ID_PAIR = ids(Y)
ID_RS = ids(J, 2, Y // 2)
ID_Z = ids(J, ZL - 1)
ID_AG = ids(J, 2, Y // 2)
ID_PAG = ids(Y, J)
ID_KZ = ids(ZH - 1)
ID_KX = ids(4, X - 1)
ID_PX = ids(X - 1)
ID_PZ = ids(ZH - 1)
N_REMOTE = ids.n

loc = Ids()
L_STALE, L_W, L_TOK, L_ANCHOR, L_MOM, L_KG = (loc(1)() for _ in range(6))
N_LOCAL = loc.n


def kernel(
    tok_ref, w_ref, kg_ref, anchor_ref, mom_ref, stale_ref,
    keys, ig, nbuf, nm, fbuf,
    stale, wv, tok, anchor, mom, pair, acc, rs, zbuf, full, pre,
    kg, part, xbuf, ksum, zb,
    ss, rr, ls, entered,
):
    w = lax.axis_index("worker")
    f = lax.axis_index("fsdp")
    c, zl, y = w % C, (w // C) % ZL, w // (C * ZL)
    x, zh = f % X, f // X

    def dev(y=y, zl=zl, c=c, zh=zh, x=x):
        return ((y * ZL + zl) * C + c, zh * X + x)

    def wrap(v, n):
        return (v + n) % n

    partner = dev(c=1 - c)
    ynext = {1: dev(y=wrap(y + 1, Y)), -1: dev(y=wrap(y - 1, Y))}
    zpeer = [dev(zl=wrap(zl + k, ZL)) for k in range(1, ZL)]
    xpeer = [dev(x=wrap(x + k, X)) for k in range(1, X)]

    column = y + zl + c + x

    def rank(zh):
        return 2 * zh + jnp.where(column + zh == 0, 5, 0)

    others = [wrap(zh + k, ZH) for k in range(1, ZH)]
    hpeer = [dev(zh=at) for at in others]
    lower = [rank(at) < rank(zh) for at in others]
    n_lower = sum(jnp.where(low, 1, 0) for low in lower)

    barrier = pltpu.get_barrier_semaphore()
    peers = [partner, ynext[1], ynext[-1], *zpeer, *xpeer]
    for peer in peers:
        pl.semaphore_signal(barrier, inc=1, device_id=peer, device_id_type=MESH)
    for k in range(ZH - 1):

        @pl.when(jnp.logical_not(lower[k]))
        def _():
            pl.semaphore_signal(barrier, inc=1, device_id=hpeer[k], device_id_type=MESH)

    def load(src, dst, at):
        copy = pltpu.make_async_copy(src, dst, ls.at[at])
        copy.start()
        return copy

    h0, h1 = pl.multiple_of(c * HALF, HALF), pl.multiple_of((1 - c) * HALF, HALF)
    c_stale = load(stale_ref.at[0], stale, L_STALE)
    c_w = load(w_ref.at[0], wv, L_W)
    c_tok = load(tok_ref, tok, L_TOK)
    c_kg = load(kg_ref, kg.at[f], L_KG)
    c_anchor = load(anchor_ref, anchor, L_ANCHOR)
    c_mom = load(mom_ref, mom, L_MOM)

    sent = []

    def send(src, dst, at, to):
        copy = pltpu.make_async_remote_copy(
            src_ref=src, dst_ref=dst, send_sem=ss.at[at], recv_sem=rr.at[at],
            device_id=to, device_id_type=MESH,
        )
        copy.start()
        sent.append(copy)

    def got(dst, at):
        pltpu.make_async_remote_copy(
            src_ref=dst, dst_ref=dst, send_sem=ss.at[at], recv_sem=rr.at[at],
            device_id=partner, device_id_type=MESH,
        ).wait_recv()

    pl.semaphore_wait(barrier, len(peers) + n_lower)

    order = [Y // 2] + [s * k for k in range(Y // 2 - 1, 0, -1) for s in (1, -1)] + [0]

    def chunk(o):
        return pl.multiple_of(wrap(y + o, Y) * CH, CH)

    for i, o in enumerate(order):
        at = chunk(o)
        send(stale_ref.at[0, pl.ds(h1 + at, CH)], pair.at[pl.ds(at, CH)], ID_PAIR(i), partner)

    c_stale.wait()

    def hops(j, way):
        return Y // 2 if (j % 2 == 0) == (way == 1) else Y // 2 - 1

    def slot(j, way, s):
        return rs.at[j, 0 if way == 1 else 1, s]

    def rid(ident, j, way, s):
        return ident(j, 0 if way == 1 else 1, s)

    long_first = [(j, way) for n in (Y // 2, Y // 2 - 1) for j in range(J) for way in (1, -1) if hops(j, way) == n]
    for i, o in enumerate(order):
        at = chunk(o)
        got(pair.at[pl.ds(at, CH)], ID_PAIR(i))
        acc[pl.ds(at, CH), :] = stale[pl.ds(h0 + at, CH), :].astype(F32) + pair[pl.ds(at, CH), :].astype(F32)
        for j, way in long_first:
            if hops(j, way) * way == o or (o == Y // 2 and hops(j, way) == o):
                send(acc.at[pl.ds(at + j * R, R)], slot(j, way, 0), rid(ID_RS, j, way, 0), ynext[way])

    def kz(k):
        copy = pltpu.make_async_remote_copy(
            src_ref=kg_ref, dst_ref=kg.at[f], send_sem=ss.at[ID_KZ(k)], recv_sem=rr.at[ID_KZ(k)],
            device_id=hpeer[k], device_id_type=MESH,
        )
        return copy

    for k in range(ZH - 1):

        @pl.when(lower[k])
        def _():
            pl.semaphore_signal(entered, inc=1, device_id=hpeer[k], device_id_type=MESH)
            kz(k).start()

        sent.append(kz(k))
    for k in range(X - 1):
        send(kg_ref, kg.at[f], ID_KX(0, k), xpeer[k])

    c_w.wait()
    c_tok.wait()
    for b in range(2):
        half = jnp.dot(tok[b * 128 : b * 128 + 128, :], wv[...], preferred_element_type=F32)
        for i in range(8):
            at = b * 8 + i
            part[at % X, at // X] = half[i * SH : (i + 1) * SH]
    for k in range(X - 1):
        send(part.at[wrap(x + k + 1, X)], xbuf.at[k], ID_PX(k), xpeer[k])

    for s in range(1, Y // 2):
        for j, way in long_first:
            n = hops(j, way)
            if s < n:
                mine = slot(j, way, s - 1)
                got(mine, rid(ID_RS, j, way, s - 1))
                mine[...] = mine[...] + acc[pl.ds(chunk(way * (n - s)) + j * R, R), :]
                send(mine, slot(j, way, s), rid(ID_RS, j, way, s), ynext[way])

    for j in range(J):
        total = acc[pl.ds(chunk(0) + j * R, R), :]
        for way in (1, -1):
            n = hops(j, way)
            got(slot(j, way, n - 1), rid(ID_RS, j, way, n - 1))
            total = total + slot(j, way, n - 1)[...]
        zbuf[j, zl] = total
        for k in range(ZL - 1):
            send(zbuf.at[j, zl], zbuf.at[j, zl], ID_Z(j, k), zpeer[k])

    for k in range(X - 1):
        got(xbuf.at[k], ID_PX(k))
    for i in range(ZH):
        ksum[i] = (part[x, i] + xbuf[0, i]) + (xbuf[1, i] + xbuf[2, i])

    @pl.when(n_lower < ZH - 1)
    def _():
        pl.semaphore_wait(entered, ZH - 1 - n_lower)

    for k in range(ZH - 1):

        @pl.when(jnp.logical_not(lower[k]))
        def _():
            kz(k).start()

    for k in range(ZH - 1):
        send(ksum.at[others[k]], zb.at[k], ID_PZ(k), hpeer[k])
    for k in range(ZH - 1):
        at = wrap(zh - k - 1, ZH) * X + x
        got(kg.at[at], ID_KZ(k))
        for i in range(X - 1):
            send(kg.at[at], kg.at[at], ID_KX(k + 1, i), xpeer[i])

    def place(core, o, j):
        return pl.ds(pl.multiple_of(core * HALF + chunk(o) + j * R, R), R)

    for j in range(J):
        for k in range(ZL - 1):
            got(zbuf.at[j, wrap(zl - k - 1, ZL)], ID_Z(j, k))
        here = place(c, 0, j)
        full[here, :] = ((zbuf[j, 0] + zbuf[j, 1]) + (zbuf[j, 2] + zbuf[j, 3])) * (1.0 / WORKERS)
        for way in (1, -1):
            send(full.at[here], full.at[here], rid(ID_AG, j, way, 0), ynext[way])
        send(full.at[here], full.at[here], ID_PAG(0, j), partner)

    for rel in range(ZH):
        for k in range(X - 1):
            at = wrap(zh - rel, ZH) * X + wrap(x - k - 1, X)
            got(kg.at[at], ID_KX(rel, k))
    c_kg.wait()
    portion = kg[...].reshape(TOK, KW)
    for b in range(2):
        ig[b * 128 : b * 128 + 128, :] = lax.dot_general(
            portion[b * 128 : b * 128 + 128], wv[...], (((1,), (1,)), ((), ())), preferred_element_type=F32
        ).astype(BF16)
    c_anchor.wait()
    c_mom.wait()
    for b in range(4):
        rows = slice(b * 128, b * 128 + 128)
        grad = lax.dot_general(
            tok[:, rows], portion, (((0,), (0,)), ((), ())), preferred_element_type=F32
        )
        fresh = anchor[rows, :] - (wv[rows, :].astype(F32) - inner_rate * grad)
        fbuf[0, rows, :] = fresh.astype(BF16)
        pre[rows, :] = anchor[rows, :] - outer_rate * (
            outer_momentum * outer_momentum * mom[rows, :] + (fresh - stale[rows, :].astype(F32)) * (1.0 / WORKERS)
        )

    def finish(core, o):
        rows = pl.ds(pl.multiple_of(core * HALF + chunk(o), CH), CH)
        nbuf[0, rows, :] = (pre[rows, :] - (outer_rate * (1.0 + outer_momentum)) * full[rows, :]).astype(BF16)

    finish(c, 0)
    for s in range(Y // 2):
        for j, way in long_first:
            n = hops(j, way)
            if s < n:
                o = -way * (s + 1)
                here = place(c, o, j)
                got(full.at[here], rid(ID_AG, j, way, s))
                if s + 1 < n:
                    send(full.at[here], full.at[here], rid(ID_AG, j, way, s + 1), ynext[way])
                send(full.at[here], full.at[here], ID_PAG(o % Y, j), partner)
        for o in (s + 1, -s - 1) if s + 1 < Y // 2 else (s + 1,):
            finish(c, o)
        for o in (s, -s) if s else (0,):
            for j in range(J):
                got(full.at[place(1 - c, o, j)], ID_PAG(o % Y, j))
            finish(1 - c, o)
    for k in range(ZH - 1):
        got(zb.at[k], ID_PZ(k))
    keys[...] = ((ksum[zh] + zb[0]) + (zb[1] + zb[2])).astype(BF16)
    for j in range(J):
        got(full.at[place(1 - c, Y // 2, j)], ID_PAG(Y // 2, j))
    finish(1 - c, Y // 2)
    share = pl.ds(pl.multiple_of(w * 8, 8), 8)
    nm[...] = outer_momentum * mom[share, :] + full[share, :]

    for copy in sent:
        copy.wait_send()


def write(*refs):
    n = len(refs) // 2
    copies = [pltpu.make_async_copy(a, b, refs[-1].at[i]) for i, (a, b) in enumerate(zip(refs[:n], refs[n:-1]))]
    for copy in copies:
        copy.start()
    for copy in copies:
        copy.wait()


def local(*args):
    scratch = [
        pltpu.VMEM((ROWS, KW), BF16),
        pltpu.VMEM((ROWS, KW), BF16),
        pltpu.VMEM((TOK, ROWS), BF16),
        pltpu.VMEM((ROWS, KW), F32),
        pltpu.VMEM((ROWS, KW), F32),
        pltpu.VMEM((HALF, KW), BF16),
        pltpu.VMEM((HALF, KW), F32),
        pltpu.VMEM((J, 2, Y // 2, R, KW), F32),
        pltpu.VMEM((J, ZL, R, KW), F32),
        pltpu.VMEM((ROWS, KW), F32),
        pltpu.VMEM((ROWS, KW), F32),
        pltpu.VMEM((ZH * X, SH, KW), BF16),
        pltpu.VMEM((X, ZH, SH, KW), F32),
        pltpu.VMEM((X - 1, ZH, SH, KW), F32),
        pltpu.VMEM((ZH, SH, KW), F32),
        pltpu.VMEM((3, SH, KW), F32),
        pltpu.SemaphoreType.DMA((N_REMOTE,)),
        pltpu.SemaphoreType.DMA((N_REMOTE,)),
        pltpu.SemaphoreType.DMA((N_LOCAL,)),
        pltpu.SemaphoreType.REGULAR,
    ]
    hbm = pl.BlockSpec(memory_space=pl.ANY)
    vmem = pl.BlockSpec(memory_space=pltpu.VMEM)
    shapes = (
        jax.ShapeDtypeStruct((SH, KW), BF16),
        jax.ShapeDtypeStruct((TOK, ROWS), BF16),
        jax.ShapeDtypeStruct((1, ROWS, KW), BF16),
        jax.ShapeDtypeStruct((8, KW), F32),
        jax.ShapeDtypeStruct((1, ROWS, KW), BF16),
    )
    results = pl.pallas_call(
        kernel,
        out_shape=shapes,
        in_specs=[hbm] * 6,
        out_specs=(vmem,) * 5,
        scratch_shapes=scratch,
        compiler_params=pltpu.CompilerParams(
            collective_id=0, has_side_effects=True, vmem_limit_bytes=VMEM_LIMIT
        ),
    )(*args)
    return pl.pallas_call(
        write,
        out_shape=shapes,
        in_specs=[vmem] * 5,
        out_specs=(hbm,) * 5,
        scratch_shapes=[pltpu.SemaphoreType.DMA((5,))],
        compiler_params=pltpu.CompilerParams(vmem_limit_bytes=4 * 1024 * 1024),
    )(*results)


def solution(mesh):
    in_specs = (
        P("worker", "fsdp"),
        P("worker", "fsdp", None),
        P(("worker", "fsdp"), None),
        P("fsdp", None),
        P("fsdp", None),
        P("worker", "fsdp", None),
    )
    out_specs = (
        P(("worker", "fsdp"), None),
        P("worker", "fsdp"),
        P("worker", "fsdp", None),
        P(("fsdp", "worker"), None),
        P("worker", "fsdp", None),
    )
    return jax.shard_map(local, mesh=mesh, in_specs=in_specs, out_specs=out_specs, check_vma=False)
```

time: 64.7 us -> 66.4 us (1.026)
  Pallas kernels: 58.6 us -> 63.8 us
  local copies, waits for them, and re-layouts: 5.25 us -> 1.66 us
    pallas_call x1 -> x2, Pallas kernels: 58.6 us -> 63.8 us  [the longest x1 62.7 us: local(): pl.pallas_call(kernel, out_shape=shapes, in_specs=[hbm] * 6, out_specs=(v...]
    unnamed x11 -> x4, local copies, waits for them, and re-layouts: 5.25 us -> 1.66 us
where the time goes in v2:
time: 66.4 us; the launch traced here: 66.1 us
  Pallas kernels  63.8 us (96%)
  local copies, waits for them, and re-layouts  1.66 us (2%)
    pallas_call x1, Pallas kernels, local(): pl.pallas_call(kernel, out_shape=shapes, in_specs=[hbm] * 6, out_specs=(v...  62.7 us
    unnamed x4, local copies, waits for them, and re-layouts  1.66 us

profile of v2, /device:TPU:1, one launch (start us, length us, event | category | flops | bytes accessed | tf_op | source)
XLA Modules:
  0.0 66.1 jit_solution(9336591965996242117)
XLA Ops:
  0.6 0.0 copy-start
  0.6 0.9 %copy-done = bf16[256,512]{1,0:T(8,128)(2,1)S(1)} copy-done((bf16[256,512]{1,0:T(8,128)(2,1)S(1)}, bf16[256,512]{1,0:T(8,128)(2,1)}, u32[]{:S(2)}) %copy-start) | copy-done | bytes 262168
  1.6 0.0 copy-start.1
  1.6 0.7 %copy-done.1 = bf16[16,512]{1,0:T(8,128)(2,1)S(1)} copy-done((bf16[16,512]{1,0:T(8,128)(2,1)S(1)}, bf16[16,512]{1,0:T(8,128)(2,1)}, u32[]{:S(2)}) %copy-start.1) | copy-done | bytes 16408
  2.3 62.7 %shard_map.101 = (bf16[16,512]{1,0:T(8,128)(2,1)S(1)}, bf16[256,512]{1,0:T(8,128)(2,1)S(1)}, bf16[1,512,512]{2,1,0:T(8,128)(2,1)S(1)}, f32[8,512]{1,0:T(8,128)S(1)}, bf16[1,512,512]{2,1,0:T(8,128)(2,1)S(1)}) custom-call(bf16[256,512]{1,0:T(8,128)(2,1)S(1)} %copy-done, bf16[1,512,512]{2,1,0:T(8,128)(2,1)} %w_ref.1, bf16[16,512]{1,0:T(8,128)(2,1)S(1)} %copy-done.1, ...), custom_call_target="tpu_custom_call" | custom-call | tf_op jit(solution)/shard_map/pallas_call | solution.py:348
  65.0 1.1 %shard_map.102 = (bf16[16,512]{1,0:T(8,128)(2,1)}, bf16[256,512]{1,0:T(8,128)(2,1)}, bf16[1,512,512]{2,1,0:T(8,128)(2,1)}, f32[8,512]{1,0:T(8,128)}, bf16[1,512,512]{2,1,0:T(8,128)(2,1)}) custom-call(bf16[16,512]{1,0:T(8,128)(2,1)S(1)} %get-tuple-element.10.refs_0_, bf16[256,512]{1,0:T(8,128)(2,1)S(1)} %get-tuple-element.11.refs_1_, ...), custom_call_target="tpu_custom_call" | custom-call | tf_op jit(solution)/shard_map/pallas_call | solution.py:358
Async XLA Ops:
  0.6 1.0 %copy-start = (bf16[256,512]{1,0:T(8,128)(2,1)S(1)}, bf16[256,512]{1,0:T(8,128)(2,1)}, u32[]{:S(2)}) copy-start(bf16[256,512]{1,0:T(8,128)(2,1)} %tok_ref.1) | copy-start | bytes 786436
  1.6 0.7 %copy-start.1 = (bf16[16,512]{1,0:T(8,128)(2,1)S(1)}, bf16[16,512]{1,0:T(8,128)(2,1)}, u32[]{:S(2)}) copy-start(bf16[16,512]{1,0:T(8,128)(2,1)} %kg_ref.1) | copy-start | bytes 49156

commit v3 on v2

--- a/solution.py
+++ b/solution.py
@@ -17,7 +17,7 @@
 J = 2
 R = CH // J
 SH = 16
-VMEM_LIMIT = 53400 * 1024
+VMEM_LIMIT = 40 * 1024 * 1024
 F32, BF16 = jnp.float32, jnp.bfloat16
 MESH = pl.DeviceIdType.MESH
 
@@ -67,7 +67,7 @@
     keys, ig, nbuf, nm, fbuf,
     stale, wv, tok, anchor, mom, pair, acc, rs, zbuf, full, pre,
     kg, part, xbuf, ksum, zb,
-    ss, rr, ls, entered,
+    ss, rr, ls, ans_c, ans_y, ans_z, ans_x, ans_h,
 ):
     w = lax.axis_index("worker")
     f = lax.axis_index("fsdp")
@@ -85,25 +85,42 @@
     zpeer = [dev(zl=wrap(zl + k, ZL)) for k in range(1, ZL)]
     xpeer = [dev(x=wrap(x + k, X)) for k in range(1, X)]
 
-    column = y + zl + c + x
-
-    def rank(zh):
-        return 2 * zh + jnp.where(column + zh == 0, 5, 0)
-
-    others = [wrap(zh + k, ZH) for k in range(1, ZH)]
-    hpeer = [dev(zh=at) for at in others]
-    lower = [rank(at) < rank(zh) for at in others]
-    n_lower = sum(jnp.where(low, 1, 0) for low in lower)
+    zat = [wrap(zl + k, ZL) for k in range(1, ZL)]
+    xat = [wrap(x + k, X) for k in range(1, X)]
+    hat = [wrap(zh + k, ZH) for k in range(1, ZH)]
+    hpeer = [dev(zh=at) for at in hat]
+    lower = [at < zh for at in hat]
+
+    odd = y % 2 == 1
+    relations = [(partner, c == 1, ans_c)]
+    relations += [(ynext[way], odd, ans_y.at[0 if way == -1 else 1]) for way in (1, -1)]
+    relations += [(peer, at < zl, ans_z) for peer, at in zip(zpeer, zat)]
+    relations += [(peer, at < x, ans_x) for peer, at in zip(xpeer, xat)]
+    relations += [(peer, at > zh, ans_h) for peer, at in zip(hpeer, hat)]
+    n_greeted = (1 - c) + 2 * (1 - y % 2) + (ZL - 1 - zl) + (X - 1 - x) + zh
 
     barrier = pltpu.get_barrier_semaphore()
-    peers = [partner, ynext[1], ynext[-1], *zpeer, *xpeer]
-    for peer in peers:
-        pl.semaphore_signal(barrier, inc=1, device_id=peer, device_id_type=MESH)
-    for k in range(ZH - 1):
-
-        @pl.when(jnp.logical_not(lower[k]))
+    for peer, greets, _ in relations:
+
+        @pl.when(greets)
         def _():
-            pl.semaphore_signal(barrier, inc=1, device_id=hpeer[k], device_id_type=MESH)
+            pl.semaphore_signal(barrier, inc=1, device_id=peer, device_id_type=MESH)
+
+    def enter():
+        @pl.when(n_greeted > 0)
+        def _():
+            pl.semaphore_wait(barrier, n_greeted)
+
+        for peer, greets, answer in relations:
+
+            @pl.when(jnp.logical_not(greets))
+            def _():
+                pl.semaphore_signal(answer, inc=1, device_id=peer, device_id_type=MESH)
+
+    def answered(sem, n):
+        @pl.when(n > 0)
+        def _():
+            pl.semaphore_wait(sem, n)
 
     def load(src, dst, at):
         copy = pltpu.make_async_copy(src, dst, ls.at[at])
@@ -134,7 +151,8 @@
             device_id=partner, device_id_type=MESH,
         ).wait_recv()
 
-    pl.semaphore_wait(barrier, len(peers) + n_lower)
+    enter()
+    answered(ans_c, c)
 
     order = [Y // 2] + [s * k for k in range(Y // 2 - 1, 0, -1) for s in (1, -1)] + [0]
 
@@ -157,12 +175,16 @@
         return ident(j, 0 if way == 1 else 1, s)
 
     long_first = [(j, way) for n in (Y // 2, Y // 2 - 1) for j in range(J) for way in (1, -1) if hops(j, way) == n]
+    ways = [1, -1]
     for i, o in enumerate(order):
         at = chunk(o)
         got(pair.at[pl.ds(at, CH)], ID_PAIR(i))
         acc[pl.ds(at, CH), :] = stale[pl.ds(h0 + at, CH), :].astype(F32) + pair[pl.ds(at, CH), :].astype(F32)
         for j, way in long_first:
             if hops(j, way) * way == o or (o == Y // 2 and hops(j, way) == o):
+                if way in ways:
+                    ways.remove(way)
+                    answered(ans_y.at[0 if way == 1 else 1], y % 2)
                 send(acc.at[pl.ds(at + j * R, R)], slot(j, way, 0), rid(ID_RS, j, way, 0), ynext[way])
 
     def kz(k):
@@ -176,12 +198,9 @@
 
         @pl.when(lower[k])
         def _():
-            pl.semaphore_signal(entered, inc=1, device_id=hpeer[k], device_id_type=MESH)
             kz(k).start()
 
         sent.append(kz(k))
-    for k in range(X - 1):
-        send(kg_ref, kg.at[f], ID_KX(0, k), xpeer[k])
 
     c_w.wait()
     c_tok.wait()
@@ -190,8 +209,6 @@
         for i in range(8):
             at = b * 8 + i
             part[at % X, at // X] = half[i * SH : (i + 1) * SH]
-    for k in range(X - 1):
-        send(part.at[wrap(x + k + 1, X)], xbuf.at[k], ID_PX(k), xpeer[k])
 
     for s in range(1, Y // 2):
         for j, way in long_first:
@@ -201,7 +218,14 @@
                 got(mine, rid(ID_RS, j, way, s - 1))
                 mine[...] = mine[...] + acc[pl.ds(chunk(way * (n - s)) + j * R, R), :]
                 send(mine, slot(j, way, s), rid(ID_RS, j, way, s), ynext[way])
-
+        if s == 1:
+            answered(ans_x, x)
+            for k in range(X - 1):
+                send(kg_ref, kg.at[f], ID_KX(0, k), xpeer[k])
+            for k in range(X - 1):
+                send(part.at[xat[k]], xbuf.at[k], ID_PX(k), xpeer[k])
+
+    answered(ans_z, zl)
     for j in range(J):
         total = acc[pl.ds(chunk(0) + j * R, R), :]
         for way in (1, -1):
@@ -216,11 +240,7 @@
         got(xbuf.at[k], ID_PX(k))
     for i in range(ZH):
         ksum[i] = (part[x, i] + xbuf[0, i]) + (xbuf[1, i] + xbuf[2, i])
-
-    @pl.when(n_lower < ZH - 1)
-    def _():
-        pl.semaphore_wait(entered, ZH - 1 - n_lower)
-
+    answered(ans_h, ZH - 1 - zh)
     for k in range(ZH - 1):
 
         @pl.when(jnp.logical_not(lower[k]))
@@ -228,7 +248,7 @@
             kz(k).start()
 
     for k in range(ZH - 1):
-        send(ksum.at[others[k]], zb.at[k], ID_PZ(k), hpeer[k])
+        send(ksum.at[hat[k]], zb.at[k], ID_PZ(k), hpeer[k])
     for k in range(ZH - 1):
         at = wrap(zh - k - 1, ZH) * X + x
         got(kg.at[at], ID_KZ(k))
@@ -257,9 +277,8 @@
         ig[b * 128 : b * 128 + 128, :] = lax.dot_general(
             portion[b * 128 : b * 128 + 128], wv[...], (((1,), (1,)), ((), ())), preferred_element_type=F32
         ).astype(BF16)
-    c_anchor.wait()
-    c_mom.wait()
-    for b in range(4):
+
+    def products(b):
         rows = slice(b * 128, b * 128 + 128)
         grad = lax.dot_general(
             tok[:, rows], portion, (((0,), (0,)), ((), ())), preferred_element_type=F32
@@ -274,7 +293,6 @@
         rows = pl.ds(pl.multiple_of(core * HALF + chunk(o), CH), CH)
         nbuf[0, rows, :] = (pre[rows, :] - (outer_rate * (1.0 + outer_momentum)) * full[rows, :]).astype(BF16)
 
-    finish(c, 0)
     for s in range(Y // 2):
         for j, way in long_first:
             n = hops(j, way)
@@ -285,18 +303,27 @@
                 if s + 1 < n:
                     send(full.at[here], full.at[here], rid(ID_AG, j, way, s + 1), ynext[way])
                 send(full.at[here], full.at[here], ID_PAG(o % Y, j), partner)
-        for o in (s + 1, -s - 1) if s + 1 < Y // 2 else (s + 1,):
-            finish(c, o)
-        for o in (s, -s) if s else (0,):
-            for j in range(J):
-                got(full.at[place(1 - c, o, j)], ID_PAG(o % Y, j))
-            finish(1 - c, o)
+        if s == 0:
+            c_anchor.wait()
+            c_mom.wait()
+        if s < 2:
+            products(2 * s)
+            products(2 * s + 1)
+        if s == 2:
+            for o in (0, 1, -1, 2, -2, 3, -3):
+                finish(c, o)
+            for o in (0, 1, -1, 2, -2):
+                for j in range(J):
+                    got(full.at[place(1 - c, o, j)], ID_PAG(o % Y, j))
+                finish(1 - c, o)
     for k in range(ZH - 1):
         got(zb.at[k], ID_PZ(k))
     keys[...] = ((ksum[zh] + zb[0]) + (zb[1] + zb[2])).astype(BF16)
-    for j in range(J):
-        got(full.at[place(1 - c, Y // 2, j)], ID_PAG(Y // 2, j))
-    finish(1 - c, Y // 2)
+    finish(c, Y // 2)
+    for o in (3, -3, Y // 2):
+        for j in range(J):
+            got(full.at[place(1 - c, o, j)], ID_PAG(o % Y, j))
+        finish(1 - c, o)
     share = pl.ds(pl.multiple_of(w * 8, 8), 8)
     nm[...] = outer_momentum * mom[share, :] + full[share, :]
 
@@ -314,6 +341,7 @@
 
 
 def local(*args):
+    args = [pltpu.with_memory_space_constraint(a, pltpu.HBM) for a in args]
     scratch = [
         pltpu.VMEM((ROWS, KW), BF16),
         pltpu.VMEM((ROWS, KW), BF16),
@@ -334,6 +362,10 @@
         pltpu.SemaphoreType.DMA((N_REMOTE,)),
         pltpu.SemaphoreType.DMA((N_REMOTE,)),
         pltpu.SemaphoreType.DMA((N_LOCAL,)),
+        pltpu.SemaphoreType.REGULAR,
+        pltpu.SemaphoreType.REGULAR((2,)),
+        pltpu.SemaphoreType.REGULAR,
+        pltpu.SemaphoreType.REGULAR,
         pltpu.SemaphoreType.REGULAR,
     ]
     hbm = pl.BlockSpec(memory_space=pl.ANY)

time: 66.4 us -> 52.4 us (0.79)
  the two profiles are of different devices: /device:TPU:1 before, /device:TPU:833 now
where the time goes in v3:
time: 52.4 us; the launch traced here: 52.3 us
  Pallas kernels  51.7 us (99%)
  between operations  0.64 us (1%)
    pallas_call x1, Pallas kernels, local(): pl.pallas_call(kernel, out_shape=shapes, in_specs=[hbm] * 6, out_specs=(v...  50.6 us
    pallas_call x1, Pallas kernels, local(): pl.pallas_call(write, out_shape=shapes, in_specs=[vmem] * 5, out_specs=(h...  1.11 us

profile of v3, /device:TPU:833, one launch (start us, length us, event | category | flops | bytes accessed | tf_op | source)
XLA Modules:
  0.0 52.3 jit_solution(17101529757165836893)
XLA Ops:
  0.6 50.6 %shard_map.101 = (bf16[16,512]{1,0:T(8,128)(2,1)S(1)}, bf16[256,512]{1,0:T(8,128)(2,1)S(1)}, bf16[1,512,512]{2,1,0:T(8,128)(2,1)S(1)}, f32[8,512]{1,0:T(8,128)S(1)}, bf16[1,512,512]{2,1,0:T(8,128)(2,1)S(1)}) custom-call(bf16[256,512]{1,0:T(8,128)(2,1)} %tok_ref.1, bf16[1,512,512]{2,1,0:T(8,128)(2,1)} %w_ref.1, bf16[16,512]{1,0:T(8,128)(2,1)} %kg_ref.1, ...), custom_call_target="tpu_custom_call" | custom-call | tf_op jit(solution)/shard_map/pallas_call | solution.py:380
  51.2 1.1 %shard_map.102 = (bf16[16,512]{1,0:T(8,128)(2,1)}, bf16[256,512]{1,0:T(8,128)(2,1)}, bf16[1,512,512]{2,1,0:T(8,128)(2,1)}, f32[8,512]{1,0:T(8,128)}, bf16[1,512,512]{2,1,0:T(8,128)(2,1)}) custom-call(bf16[16,512]{1,0:T(8,128)(2,1)S(1)} %get-tuple-element.10.refs_0_, bf16[256,512]{1,0:T(8,128)(2,1)S(1)} %get-tuple-element.11.refs_1_, ...), custom_call_target="tpu_custom_call" | custom-call | tf_op jit(solution)/shard_map/pallas_call | solution.py:390

commit v4 on v3

--- a/solution.py
+++ b/solution.py
@@ -48,7 +48,7 @@
 ids = Ids()
 ID_PAIR = ids(Y)
 ID_RS = ids(J, 2, Y // 2)
-ID_Z = ids(J, ZL - 1)
+ID_Z = ids(J, ZL)
 ID_AG = ids(J, 2, Y // 2)
 ID_PAG = ids(Y, J)
 ID_KZ = ids(ZH - 1)
@@ -89,6 +89,9 @@
     xat = [wrap(x + k, X) for k in range(1, X)]
     hat = [wrap(zh + k, ZH) for k in range(1, ZH)]
     hpeer = [dev(zh=at) for at in hat]
+    low = zl < ZL // 2
+    end = jnp.where(low, ZL - 1, 0)
+    zfar = [end, jnp.where(zl == 0, 2, jnp.where(zl == 1, 0, jnp.where(zl == 2, 3, 1))), jnp.where(low, zl + 1, zl - 1)]
     lower = [at < zh for at in hat]
 
     odd = y % 2 == 1
@@ -111,7 +114,8 @@
         def _():
             pl.semaphore_wait(barrier, n_greeted)
 
-        for peer, greets, answer in relations:
+    def answer_to(some):
+        for peer, greets, answer in some:
 
             @pl.when(jnp.logical_not(greets))
             def _():
@@ -137,9 +141,9 @@
 
     sent = []
 
-    def send(src, dst, at, to):
+    def send(src, dst, at, to, recv_at=None):
         copy = pltpu.make_async_remote_copy(
-            src_ref=src, dst_ref=dst, send_sem=ss.at[at], recv_sem=rr.at[at],
+            src_ref=src, dst_ref=dst, send_sem=ss.at[at], recv_sem=rr.at[at if recv_at is None else recv_at],
             device_id=to, device_id_type=MESH,
         )
         copy.start()
@@ -152,6 +156,7 @@
         ).wait_recv()
 
     enter()
+    answer_to(relations[:3])
     answered(ans_c, c)
 
     order = [Y // 2] + [s * k for k in range(Y // 2 - 1, 0, -1) for s in (1, -1)] + [0]
@@ -162,6 +167,8 @@
     for i, o in enumerate(order):
         at = chunk(o)
         send(stale_ref.at[0, pl.ds(h1 + at, CH)], pair.at[pl.ds(at, CH)], ID_PAIR(i), partner)
+
+    answer_to(relations[3:])
 
     c_stale.wait()
 
@@ -194,7 +201,7 @@
         )
         return copy
 
-    for k in range(ZH - 1):
+    for k in (1, 0, 2):
 
         @pl.when(lower[k])
         def _():
@@ -234,21 +241,15 @@
             total = total + slot(j, way, n - 1)[...]
         zbuf[j, zl] = total
         for k in range(ZL - 1):
-            send(zbuf.at[j, zl], zbuf.at[j, zl], ID_Z(j, k), zpeer[k])
-
-    for k in range(X - 1):
-        got(xbuf.at[k], ID_PX(k))
-    for i in range(ZH):
-        ksum[i] = (part[x, i] + xbuf[0, i]) + (xbuf[1, i] + xbuf[2, i])
+            send(zbuf.at[j, zl], zbuf.at[j, zl], ID_Z(j, k), dev(zl=zfar[k]), ID_Z(j, 0) + zl)
+
     answered(ans_h, ZH - 1 - zh)
-    for k in range(ZH - 1):
+    for k in (1, 0, 2):
 
         @pl.when(jnp.logical_not(lower[k]))
         def _():
             kz(k).start()
 
-    for k in range(ZH - 1):
-        send(ksum.at[hat[k]], zb.at[k], ID_PZ(k), hpeer[k])
     for k in range(ZH - 1):
         at = wrap(zh - k - 1, ZH) * X + x
         got(kg.at[at], ID_KZ(k))
@@ -260,12 +261,19 @@
 
     for j in range(J):
         for k in range(ZL - 1):
-            got(zbuf.at[j, wrap(zl - k - 1, ZL)], ID_Z(j, k))
+            got(zbuf.at[j, zat[k]], ID_Z(j, 0) + zat[k])
         here = place(c, 0, j)
         full[here, :] = ((zbuf[j, 0] + zbuf[j, 1]) + (zbuf[j, 2] + zbuf[j, 3])) * (1.0 / WORKERS)
         for way in (1, -1):
             send(full.at[here], full.at[here], rid(ID_AG, j, way, 0), ynext[way])
         send(full.at[here], full.at[here], ID_PAG(0, j), partner)
+
+    for k in range(X - 1):
+        got(xbuf.at[k], ID_PX(k))
+    for i in range(ZH):
+        ksum[i] = (part[x, i] + xbuf[0, i]) + (xbuf[1, i] + xbuf[2, i])
+    for k in (1, 0, 2):
+        send(ksum.at[hat[k]], zb.at[k], ID_PZ(k), hpeer[k])
 
     for rel in range(ZH):
         for k in range(X - 1):

time: 52.4 us -> 54.2 us (1.034)
  the two profiles are of different devices: /device:TPU:833 before, /device:TPU:65 now
where the time goes in v4:
time: 54.2 us; the launch traced here: 54 us
  Pallas kernels  53.4 us (99%)
  between operations  0.64 us (1%)
    pallas_call x1, Pallas kernels, local(): pl.pallas_call(kernel, out_shape=shapes, in_specs=[hbm] * 6, out_specs=(v...  52.3 us
    pallas_call x1, Pallas kernels, local(): pl.pallas_call(write, out_shape=shapes, in_specs=[vmem] * 5, out_specs=(h...  1.11 us

profile of v4, /device:TPU:65, one launch (start us, length us, event | category | flops | bytes accessed | tf_op | source)
XLA Modules:
  0.0 54.0 jit_solution(5546824927803645385)
XLA Ops:
  0.6 52.3 %shard_map.101 = (bf16[16,512]{1,0:T(8,128)(2,1)S(1)}, bf16[256,512]{1,0:T(8,128)(2,1)S(1)}, bf16[1,512,512]{2,1,0:T(8,128)(2,1)S(1)}, f32[8,512]{1,0:T(8,128)S(1)}, bf16[1,512,512]{2,1,0:T(8,128)(2,1)S(1)}) custom-call(bf16[256,512]{1,0:T(8,128)(2,1)} %tok_ref.1, bf16[1,512,512]{2,1,0:T(8,128)(2,1)} %w_ref.1, bf16[16,512]{1,0:T(8,128)(2,1)} %kg_ref.1, ...), custom_call_target="tpu_custom_call" | custom-call | tf_op jit(solution)/shard_map/pallas_call | solution.py:388
  52.9 1.1 %shard_map.102 = (bf16[16,512]{1,0:T(8,128)(2,1)}, bf16[256,512]{1,0:T(8,128)(2,1)}, bf16[1,512,512]{2,1,0:T(8,128)(2,1)}, f32[8,512]{1,0:T(8,128)}, bf16[1,512,512]{2,1,0:T(8,128)(2,1)}) custom-call(bf16[16,512]{1,0:T(8,128)(2,1)S(1)} %get-tuple-element.10.refs_0_, bf16[256,512]{1,0:T(8,128)(2,1)S(1)} %get-tuple-element.11.refs_1_, ...), custom_call_target="tpu_custom_call" | custom-call | tf_op jit(solution)/shard_map/pallas_call | solution.py:398

commit v5 on v4

--- a/solution.py
+++ b/solution.py
@@ -217,6 +217,12 @@
             at = b * 8 + i
             part[at % X, at // X] = half[i * SH : (i + 1) * SH]
 
+    answered(ans_x, x)
+    for k in range(X - 1):
+        send(kg_ref, kg.at[f], ID_KX(0, k), xpeer[k])
+    for k in range(X - 1):
+        send(part.at[xat[k]], xbuf.at[k], ID_PX(k), xpeer[k])
+
     for s in range(1, Y // 2):
         for j, way in long_first:
             n = hops(j, way)
@@ -225,12 +231,25 @@
                 got(mine, rid(ID_RS, j, way, s - 1))
                 mine[...] = mine[...] + acc[pl.ds(chunk(way * (n - s)) + j * R, R), :]
                 send(mine, slot(j, way, s), rid(ID_RS, j, way, s), ynext[way])
-        if s == 1:
-            answered(ans_x, x)
-            for k in range(X - 1):
-                send(kg_ref, kg.at[f], ID_KX(0, k), xpeer[k])
-            for k in range(X - 1):
-                send(part.at[xat[k]], xbuf.at[k], ID_PX(k), xpeer[k])
+
+    for k in range(X - 1):
+        got(xbuf.at[k], ID_PX(k))
+    for i in range(ZH):
+        ksum[i] = (part[x, i] + xbuf[0, i]) + (xbuf[1, i] + xbuf[2, i])
+
+    def pz(k):
+        return pltpu.make_async_remote_copy(
+            src_ref=ksum.at[hat[k]], dst_ref=zb.at[k], send_sem=ss.at[ID_PZ(k)], recv_sem=rr.at[ID_PZ(k)],
+            device_id=hpeer[k], device_id_type=MESH,
+        )
+
+    for k in (1, 0, 2):
+
+        @pl.when(lower[k])
+        def _():
+            pz(k).start()
+
+        sent.append(pz(k))
 
     answered(ans_z, zl)
     for j in range(J):
@@ -268,12 +287,12 @@
             send(full.at[here], full.at[here], rid(ID_AG, j, way, 0), ynext[way])
         send(full.at[here], full.at[here], ID_PAG(0, j), partner)
 
-    for k in range(X - 1):
-        got(xbuf.at[k], ID_PX(k))
-    for i in range(ZH):
-        ksum[i] = (part[x, i] + xbuf[0, i]) + (xbuf[1, i] + xbuf[2, i])
     for k in (1, 0, 2):
-        send(ksum.at[hat[k]], zb.at[k], ID_PZ(k), hpeer[k])
+
+        @pl.when(jnp.logical_not(lower[k]))
+        def _():
+            pz(k).start()
+
 
     for rel in range(ZH):
         for k in range(X - 1):

time: 54.2 us -> 50.7 us (0.935)
  the two profiles are of different devices: /device:TPU:65 before, /device:TPU:321 now
where the time goes in v5:
time: 50.7 us; the launch traced here: 50.6 us
  Pallas kernels  50 us (99%)
  between operations  0.64 us (1%)
    pallas_call x1, Pallas kernels, local(): pl.pallas_call(kernel, out_shape=shapes, in_specs=[hbm] * 6, out_specs=(v...  48.9 us
    pallas_call x1, Pallas kernels, local(): pl.pallas_call(write, out_shape=shapes, in_specs=[vmem] * 5, out_specs=(h...  1.11 us

profile of v5, /device:TPU:321, one launch (start us, length us, event | category | flops | bytes accessed | tf_op | source)
XLA Modules:
  0.0 50.6 jit_solution(14249388406184266139)
XLA Ops:
  0.6 48.9 %shard_map.101 = (bf16[16,512]{1,0:T(8,128)(2,1)S(1)}, bf16[256,512]{1,0:T(8,128)(2,1)S(1)}, bf16[1,512,512]{2,1,0:T(8,128)(2,1)S(1)}, f32[8,512]{1,0:T(8,128)S(1)}, bf16[1,512,512]{2,1,0:T(8,128)(2,1)S(1)}) custom-call(bf16[256,512]{1,0:T(8,128)(2,1)} %tok_ref.1, bf16[1,512,512]{2,1,0:T(8,128)(2,1)} %w_ref.1, bf16[16,512]{1,0:T(8,128)(2,1)} %kg_ref.1, ...), custom_call_target="tpu_custom_call" | custom-call | tf_op jit(solution)/shard_map/pallas_call | solution.py:407
  49.5 1.1 %shard_map.102 = (bf16[16,512]{1,0:T(8,128)(2,1)}, bf16[256,512]{1,0:T(8,128)(2,1)}, bf16[1,512,512]{2,1,0:T(8,128)(2,1)}, f32[8,512]{1,0:T(8,128)}, bf16[1,512,512]{2,1,0:T(8,128)(2,1)}) custom-call(bf16[16,512]{1,0:T(8,128)(2,1)S(1)} %get-tuple-element.10.refs_0_, bf16[256,512]{1,0:T(8,128)(2,1)S(1)} %get-tuple-element.11.refs_1_, ...), custom_call_target="tpu_custom_call" | custom-call | tf_op jit(solution)/shard_map/pallas_call | solution.py:417

commit v6 on v5

--- a/solution.py
+++ b/solution.py
@@ -269,12 +269,6 @@
         def _():
             kz(k).start()
 
-    for k in range(ZH - 1):
-        at = wrap(zh - k - 1, ZH) * X + x
-        got(kg.at[at], ID_KZ(k))
-        for i in range(X - 1):
-            send(kg.at[at], kg.at[at], ID_KX(k + 1, i), xpeer[i])
-
     def place(core, o, j):
         return pl.ds(pl.multiple_of(core * HALF + chunk(o) + j * R, R), R)
 
@@ -294,21 +288,28 @@
             pz(k).start()
 
 
-    for rel in range(ZH):
-        for k in range(X - 1):
-            at = wrap(zh - rel, ZH) * X + wrap(x - k - 1, X)
-            got(kg.at[at], ID_KX(rel, k))
-    c_kg.wait()
-    portion = kg[...].reshape(TOK, KW)
-    for b in range(2):
-        ig[b * 128 : b * 128 + 128, :] = lax.dot_general(
-            portion[b * 128 : b * 128 + 128], wv[...], (((1,), (1,)), ((), ())), preferred_element_type=F32
-        ).astype(BF16)
+    for k in range(ZH - 1):
+        at = wrap(zh - k - 1, ZH) * X + x
+        got(kg.at[at], ID_KZ(k))
+        for i in range(X - 1):
+            send(kg.at[at], kg.at[at], ID_KX(k + 1, i), xpeer[i])
+
+    def first_products():
+        for rel in range(ZH):
+            for k in range(X - 1):
+                at = wrap(zh - rel, ZH) * X + wrap(x - k - 1, X)
+                got(kg.at[at], ID_KX(rel, k))
+        c_kg.wait()
+        portion = kg[...].reshape(TOK, KW)
+        for b in range(2):
+            ig[b * 128 : b * 128 + 128, :] = lax.dot_general(
+                portion[b * 128 : b * 128 + 128], wv[...], (((1,), (1,)), ((), ())), preferred_element_type=F32
+            ).astype(BF16)
 
     def products(b):
         rows = slice(b * 128, b * 128 + 128)
         grad = lax.dot_general(
-            tok[:, rows], portion, (((0,), (0,)), ((), ())), preferred_element_type=F32
+            tok[:, rows], kg[...].reshape(TOK, KW), (((0,), (0,)), ((), ())), preferred_element_type=F32
         )
         fresh = anchor[rows, :] - (wv[rows, :].astype(F32) - inner_rate * grad)
         fbuf[0, rows, :] = fresh.astype(BF16)
@@ -330,13 +331,13 @@
                 if s + 1 < n:
                     send(full.at[here], full.at[here], rid(ID_AG, j, way, s + 1), ynext[way])
                 send(full.at[here], full.at[here], ID_PAG(o % Y, j), partner)
-        if s == 0:
+        if s == 1:
+            first_products()
             c_anchor.wait()
             c_mom.wait()
-        if s < 2:
-            products(2 * s)
-            products(2 * s + 1)
         if s == 2:
+            for b in range(4):
+                products(b)
             for o in (0, 1, -1, 2, -2, 3, -3):
                 finish(c, o)
             for o in (0, 1, -1, 2, -2):

time: 50.7 us -> 50.5 us (level)
  no operation moved by 1% of the time
where the time goes in v6:
time: 50.5 us; the launch traced here: 50.4 us
  Pallas kernels  49.8 us (99%)
  between operations  0.64 us (1%)
    pallas_call x1, Pallas kernels, local(): pl.pallas_call(kernel, out_shape=shapes, in_specs=[hbm] * 6, out_specs=(v...  48.6 us
    pallas_call x1, Pallas kernels, local(): pl.pallas_call(write, out_shape=shapes, in_specs=[vmem] * 5, out_specs=(h...  1.11 us

profile of v6, /device:TPU:321, one launch (start us, length us, event | category | flops | bytes accessed | tf_op | source)
XLA Modules:
  0.0 50.4 jit_solution(15622904199971689429)
XLA Ops:
  0.6 48.6 %shard_map.101 = (bf16[16,512]{1,0:T(8,128)(2,1)S(1)}, bf16[256,512]{1,0:T(8,128)(2,1)S(1)}, bf16[1,512,512]{2,1,0:T(8,128)(2,1)S(1)}, f32[8,512]{1,0:T(8,128)S(1)}, bf16[1,512,512]{2,1,0:T(8,128)(2,1)S(1)}) custom-call(bf16[256,512]{1,0:T(8,128)(2,1)} %tok_ref.1, bf16[1,512,512]{2,1,0:T(8,128)(2,1)} %w_ref.1, bf16[16,512]{1,0:T(8,128)(2,1)} %kg_ref.1, ...), custom_call_target="tpu_custom_call" | custom-call | tf_op jit(solution)/shard_map/pallas_call | solution.py:408
  49.3 1.1 %shard_map.102 = (bf16[16,512]{1,0:T(8,128)(2,1)}, bf16[256,512]{1,0:T(8,128)(2,1)}, bf16[1,512,512]{2,1,0:T(8,128)(2,1)}, f32[8,512]{1,0:T(8,128)}, bf16[1,512,512]{2,1,0:T(8,128)(2,1)}) custom-call(bf16[16,512]{1,0:T(8,128)(2,1)S(1)} %get-tuple-element.10.refs_0_, bf16[256,512]{1,0:T(8,128)(2,1)S(1)} %get-tuple-element.11.refs_1_, ...), custom_call_target="tpu_custom_call" | custom-call | tf_op jit(solution)/shard_map/pallas_call | solution.py:418
